TPU v7x, 256 devices: a whole 4x4x8 slice. The times are simulated.
256 devices in a mesh: chan: 64 (over y, z, core), hour: 4 (over x).
Axes of the slice: x: 4, y: 4, z: 8, core: 2. Of those that a mesh axis runs over, the one named last changes fastest.
Arguments:
- spectra: bfloat16 [8, 2, 8192, 2560], P('hour', None, 'chan'), may hold values from -34 to 34, as said below
- partner_lists: int32 [64, 4], replicated, may hold values from -1 to 63, as said below
- partner_counts: int32 [64], replicated, may hold values from 2 to 4, as said below
Outputs:
- stacks: float32 [256, 8, 128, 256], P(('chan', 'hour'))
Inputs may be any that keep to these rules, and one draw needn't show every extreme that they name: The spectra are finite and bounded. `partner_lists`: row s lists distinct channel blocks, the first being s itself; entries from position partner_counts[s] on are -1. Within their counts, every block is listed by at most 4 rows, and some block by exactly 4. `partner_counts`: some row has exactly 4 partners.
All inputs are finite; a program needn't handle non-finite values.
Results may differ from a plain program's by a relative error of at most 0.0046.
Values may be sent and summed in bfloat16 or wider, within the bound.
A program may use at most 128 MiB of HBM per device.

v0:
```python
import math
import jax
import jax.numpy as jnp
from jax import lax
from jax.sharding import PartitionSpec as P

VS = 8
F0 = 64
NWIN = 8192
SMOOTH = 129
LAGS = 256


def whiten(real_part, imag_part):
    amplitude = jnp.sqrt(real_part * real_part + imag_part * imag_part)
    window_shape = (1,) * (amplitude.ndim - 1) + (SMOOTH,)
    padding = ((0, 0),) * (amplitude.ndim - 1) + ((SMOOTH // 2, SMOOTH // 2),)
    summed = lax.reduce_window(
        amplitude,
        jnp.zeros((), amplitude.dtype),
        lax.add,
        window_shape,
        (1,) * amplitude.ndim,
        padding,
    )
    denominator = summed / SMOOTH + 1e-06
    return (
        (real_part / denominator).astype(jnp.bfloat16),
        (imag_part / denominator).astype(jnp.bfloat16),
    )


def lag_table(band_bins):
    freq_index = jnp.arange(band_bins, dtype=jnp.int32)[:, None] + F0
    lag_index = jnp.arange(LAGS, dtype=jnp.int32)[None, :] - LAGS // 2
    lag_index = jnp.where(lag_index < 0, lag_index + NWIN, lag_index)
    phase_index = freq_index * lag_index % NWIN
    phase_angle = phase_index.astype(jnp.float32) * (2.0 * math.pi / NWIN)
    return jnp.concatenate([jnp.cos(phase_angle), -jnp.sin(phase_angle)], 0).astype(jnp.bfloat16)


def slot_onehot(partner_lists, partner_counts, receiver):
    offsets = jnp.arange(partner_lists.shape[1], dtype=jnp.int32)
    listed = (offsets[None, :] < partner_counts[:, None]) & (partner_lists == receiver)
    member = jnp.any(listed, axis=1)
    slot_rank = jnp.cumsum(member.astype(jnp.int32)) - 1
    slots = jnp.arange(partner_lists.shape[1], dtype=jnp.int32)
    return member[None, :] & (slot_rank[None, :] == slots[:, None])


def shards(spectra, partner_lists, partner_counts):
    windows, _, block_chans, band_bins = spectra.shape
    block_count = lax.axis_size("chan")
    hour_count = lax.axis_size("hour")
    values = spectra.astype(jnp.float32)
    white_re, white_im = whiten(values[:, 0], values[:, 1])
    stride = block_chans // VS
    local_sources = jnp.stack([white_re[:, ::stride, :], white_im[:, ::stride, :]], 1)
    local_sources = jnp.transpose(local_sources, (2, 0, 1, 3))
    receiver = lax.axis_index("chan")
    onehot = slot_onehot(partner_lists, partner_counts, receiver).astype(jnp.bfloat16)
    slot_total = onehot.shape[0]
    gathered = lax.all_gather(local_sources, "chan", axis=0, tiled=True)
    flattened = gathered.reshape(block_count, -1)
    chosen = jnp.dot(onehot, flattened, preferred_element_type=jnp.float32)
    chosen = chosen.reshape(slot_total, VS, windows, 2, band_bins)
    table_values = lag_table(band_bins)
    norm_scale = 1.0 / math.sqrt(4.0 * band_bins * windows * hour_count)

    def one_slot(source):
        cross_re = jnp.zeros((VS, block_chans, band_bins), jnp.float32)
        cross_im = jnp.zeros((VS, block_chans, band_bins), jnp.float32)
        for window in range(windows):
            src_real = source[:, window, 0][:, None, :]
            src_imag = source[:, window, 1][:, None, :]
            recv_real = white_re[window][None, :, :]
            recv_imag = white_im[window][None, :, :]
            cross_re = cross_re + src_real * recv_real + src_imag * recv_imag
            cross_im = cross_im + src_imag * recv_real - src_real * recv_imag
        cross = (
            jnp.concatenate([cross_re, cross_im], -1)
            .astype(jnp.bfloat16)
            .reshape(VS * block_chans, 2 * band_bins)
        )
        lagged = jnp.dot(cross, table_values, preferred_element_type=jnp.float32) * norm_scale
        return lagged.reshape(VS, block_chans, LAGS)

    partial_stacks = lax.map(one_slot, chosen)
    summed_hours = lax.psum(partial_stacks, "hour")
    share = slot_total // hour_count
    return lax.dynamic_slice_in_dim(summed_hours, lax.axis_index("hour") * share, share, 0)


def solution(mesh):
    return jax.shard_map(
        shards,
        mesh=mesh,
        in_specs=(P("hour", None, "chan", None), P(), P()),
        out_specs=P(("chan", "hour"), None, None, None),
        check_vma=False,
    )
```

profile of v0, /device:TPU:1, one launch (start us, length us, event | category | flops | bytes accessed | tf_op | source)
XLA Modules:
  0.0 464.1 jit_solution(17760751546049418316)
XLA Ops:
  6.5 3.2 copy.26
  9.8 0.3 convert_element_type.43
  10.1 2.3 copy-done
  12.4 0.8 add_sqrt_fusion
  13.3 129.2 %reduce_window.7 = f32[2,128,2560]{1,2,0:T(8,128)} reduce-window(f32[2,128,2560]{1,2,0:T(8,128)S(1)} %add_sqrt_fusion, f32[]{:T(128)} %constant.29.clone.1), window={size=1x1x129 pad=0_0x0_0x64_64}, to_apply=%region_2.0 | reduce-window | flops 83886080 | bytes 5242884 | tf_op jit(solution)/shard_map/reduce_window | solution.py:18
  142.4 4.0 divide_convert_fusion.1
  146.4 10.4 %slice.38 = bf16[2,8,2560]{1,2,0:T(8,128)(2,1)} slice(bf16[2,128,2560]{1,2,0:T(8,128)(2,1)S(1)} %get-tuple-element.90), slice={[0:2:1], [0:128:16], [0:2560:1]} | slice | bytes 163840 | tf_op jit(solution)/shard_map/slice | solution.py:58
  156.8 10.2 %slice.39 = bf16[2,8,2560]{1,2,0:T(8,128)(2,1)} slice(bf16[2,128,2560]{1,2,0:T(8,128)(2,1)S(1)} %get-tuple-element.91), slice={[0:2:1], [0:128:16], [0:2560:1]} | slice | bytes 163840 | tf_op jit(solution)/shard_map/slice | solution.py:58
  167.0 3.8 maximum_bitcast_fusion
  170.8 3.5 copy.27
  174.5 0.6 copy.30
  175.1 1.6 copy.31
  177.1 11.7 %cosine_convert_fusion = (bf16[2560,256]{1,0:T(8,128)(2,1)S(1)}, bf16[2560,256]{1,0:T(8,128)(2,1)S(1)}) fusion(s32[256]{0:T(256)S(1)} %compare_select_fusion, s32[2560]{0:T(1024)S(1)} %iota_add_fusion), kind=kLoop, calls=%fused_computation.34 | loop fusion | flops 11141120 | bytes 2632704 | tf_op jit(solution)/shard_map/convert.9
  188.8 1.7 pad_maximum_fusion
  190.5 74.7 %all-gather.2.cloned.1.call-done = bf16[512,2,2,2560]{3,2,1,0:T(2,128)(2,1)} async-done(((bf16[8,2,2,2560]{3,2,1,0:T(2,128)(2,1)}), bf16[512,2,2,2560]{3,2,1,0:T(2,128)(2,1)}) %all-gather.2.cloned.1.call-update) | async-done | bytes 10485776 | tf_op jit(solution)/shard_map/all_gather | solution.py:63
  265.2 13.0 %reshape.97 = bf16[64,81920]{1,0:T(8,128)(2,1)} reshape(bf16[512,2,2,2560]{3,2,1,0:T(2,128)(2,1)} %all-gather.2.cloned.1.call-done) | data formatting | bytes 20971520 | tf_op jit(solution)/shard_map/reshape | solution.py:64
  278.2 13.8 %dot_general.11 = bf16[8,2,2,2560,64]{3,2,1,0,4:T(2,128)(2,1)} reshape(bf16[81920,64]{0,1:T(8,128)(2,1)} %bitcast.71) | data formatting | bytes 20971520 | tf_op jit(solution)/shard_map/dot_general | solution.py:65
  292.0 16.1 %fusion.8 = f32[4,8,2,2,2560]{4,0,3,2,1:T(4,128)} fusion(bf16[8,2,2,2560,64]{3,2,1,0,4:T(2,128)(2,1)} %dot_general.11, s32[64]{0:T(128)S(1)} %add_reduce_fusion, pred[64]{0:T(512)(128)(4,1)S(1)} %fusion.14), kind=kOutput, calls=%fused_computation.19 | convolution fusion | flops 41943552 | bytes 11796800 | tf_op jit(solution)/shard_map/dot_general | solution.py:65
  308.2 51.6 %while.10 = (s32[]{:T(128)}, f32[4,8,128,256]{3,2,1,0:T(8,128)}, f32[4,8,2,2,2560]{4,0,3,2,1:T(4,128)}, bf16[2,128,2560]{2,1,0:T(8,128)(2,1)S(1)}, bf16[2,128,25...) while((s32[]{:T(128)}, f32[4,8,128,256]{3,2,1,0:T(8,128)}, ...), condition=%wide.region_4.5_spmd, body=%wide.region_3.4_spmd.sunk | while | flops 2748841984 | bytes 53281388 | solution.py:88
  308.5 1.7 constant_dynamic-slice_fusion.3
  310.2 0.2 copy.51
  310.3 0.2 fusion.28
  310.6 0.7 bitcast_convert_fusion.5
  311.3 5.8 %add_convert_fusion.2 = (bf16[8,128,2560]{2,1,0:T(8,128)(2,1)S(1)}, bf16[8,128,2560]{2,1,0:T(8,128)(2,1)S(1)}) fusion(f32[128,2560]{1,0:T(8,128)S(1)} %get-tuple-element.145, f32[8,2560]{1,0:T(8,128)S(1)} %get-tuple-element.148, f32[128,2560]{1,0:T(8,128)S(1)} %get-tuple-element.149, f32[8,2560]{1,0:T(8,128)S(1)} %get-tuple-element.150, ...), kind=kLoop, calls=%fused_computation.5.clone.1 | loop fusion | flops 41943040 | bytes 16056320 | tf_op jit(solution)/shard_map/convert.7
  317.1 3.1 fusion.29
  320.2 1.1 constant_dynamic-update-slice_fusion.2
  321.3 1.7 constant_dynamic-slice_fusion.3
  323.0 0.2 copy.51
  323.1 0.2 fusion.28
  323.4 0.7 bitcast_convert_fusion.5
  324.1 5.8 %add_convert_fusion.2 = (bf16[8,128,2560]{2,1,0:T(8,128)(2,1)S(1)}, bf16[8,128,2560]{2,1,0:T(8,128)(2,1)S(1)}) fusion(f32[128,2560]{1,0:T(8,128)S(1)} %get-tuple-element.145, f32[8,2560]{1,0:T(8,128)S(1)} %get-tuple-element.148, f32[128,2560]{1,0:T(8,128)S(1)} %get-tuple-element.149, f32[8,2560]{1,0:T(8,128)S(1)} %get-tuple-element.150, ...), kind=kLoop, calls=%fused_computation.5.clone.1 | loop fusion | flops 41943040 | bytes 16056320 | tf_op jit(solution)/shard_map/convert.7
  329.9 3.1 fusion.29
  333.0 1.1 constant_dynamic-update-slice_fusion.2
  334.1 1.7 constant_dynamic-slice_fusion.3
  335.8 0.2 copy.51
  336.0 0.2 fusion.28
  336.2 0.7 bitcast_convert_fusion.5
  336.9 5.8 %add_convert_fusion.2 = (bf16[8,128,2560]{2,1,0:T(8,128)(2,1)S(1)}, bf16[8,128,2560]{2,1,0:T(8,128)(2,1)S(1)}) fusion(f32[128,2560]{1,0:T(8,128)S(1)} %get-tuple-element.145, f32[8,2560]{1,0:T(8,128)S(1)} %get-tuple-element.148, f32[128,2560]{1,0:T(8,128)S(1)} %get-tuple-element.149, f32[8,2560]{1,0:T(8,128)S(1)} %get-tuple-element.150, ...), kind=kLoop, calls=%fused_computation.5.clone.1 | loop fusion | flops 41943040 | bytes 16056320 | tf_op jit(solution)/shard_map/convert.7
  342.7 3.1 fusion.29
  345.8 1.1 constant_dynamic-update-slice_fusion.2
  346.9 1.7 constant_dynamic-slice_fusion.3
  348.8 0.2 fusion.28
  349.1 0.7 bitcast_convert_fusion.5
  349.8 5.8 %add_convert_fusion.2 = (bf16[8,128,2560]{2,1,0:T(8,128)(2,1)S(1)}, bf16[8,128,2560]{2,1,0:T(8,128)(2,1)S(1)}) fusion(f32[128,2560]{1,0:T(8,128)S(1)} %get-tuple-element.145, f32[8,2560]{1,0:T(8,128)S(1)} %get-tuple-element.148, f32[128,2560]{1,0:T(8,128)S(1)} %get-tuple-element.149, f32[8,2560]{1,0:T(8,128)S(1)} %get-tuple-element.150, ...), kind=kLoop, calls=%fused_computation.5.clone.1 | loop fusion | flops 41943040 | bytes 16056320 | tf_op jit(solution)/shard_map/convert.7
  355.6 3.1 fusion.29
  358.6 1.1 constant_dynamic-update-slice_fusion.2
  359.8 94.6 %all-reduce.2.cloned.1.call-done = f32[4,8,128,256]{3,2,1,0:T(8,128)} async-done(((f32[4,8,128,256]{3,2,1,0:T(8,128)}), f32[4,8,128,256]{3,2,1,0:T(8,128)}) %all-reduce.2.cloned.1.call-update) | async-done | bytes 4194320 | tf_op jit(solution)/shard_map/psum | solution.py:89
  454.4 2.3 constant_dynamic-slice_fusion.1
  (36 shorter events, 0.7 us)
Async XLA Ops:
  6.5 258.7 %all-gather.2.cloned.1.call-start = ((), (), s32[]{:S(2)}) async-start(), calls=%async_computation | async-start | bytes 10649600 | tf_op jit(solution)/shard_map/all_gather | solution.py:63
  10.1 2.3 copy-start
  146.4 20.6 %copy-start.1 = (bf16[2,128,2560]{1,2,0:T(8,128)(2,1)}, bf16[2,128,2560]{1,2,0:T(8,128)(2,1)S(1)}, u32[]{:S(2)}) copy-start(bf16[2,128,2560]{1,2,0:T(8,128)(2,1)S(1)} %get-tuple-element.91) | copy-start | bytes 3932164
  174.4 280.0 %all-reduce.2.cloned.1.call-start = ((), (), s32[]{:S(2)}) async-start(), calls=%async_computation.1 | async-start | bytes 8388608 | tf_op jit(solution)/shard_map/psum | solution.py:89
  174.4 2.3 copy-start.3
  174.4 2.3 copy-start.4
  311.3 5.8 %copy-start.2 = (bf16[5120,256]{1,0:T(8,128)(2,1)S(1)}, bf16[5120,256]{1,0:T(8,128)(2,1)}, u32[]{:S(2)}) copy-start(bf16[5120,256]{1,0:T(8,128)(2,1)} %get-tuple-element.178) | copy-start | bytes 7864324 | tf_op jit(solution)/shard_map/while
  324.1 5.8 %copy-start.2 = (bf16[5120,256]{1,0:T(8,128)(2,1)S(1)}, bf16[5120,256]{1,0:T(8,128)(2,1)}, u32[]{:S(2)}) copy-start(bf16[5120,256]{1,0:T(8,128)(2,1)} %get-tuple-element.178) | copy-start | bytes 7864324 | tf_op jit(solution)/shard_map/while
  336.9 5.8 %copy-start.2 = (bf16[5120,256]{1,0:T(8,128)(2,1)S(1)}, bf16[5120,256]{1,0:T(8,128)(2,1)}, u32[]{:S(2)}) copy-start(bf16[5120,256]{1,0:T(8,128)(2,1)} %get-tuple-element.178) | copy-start | bytes 7864324 | tf_op jit(solution)/shard_map/while
  349.7 5.8 %copy-start.2 = (bf16[5120,256]{1,0:T(8,128)(2,1)S(1)}, bf16[5120,256]{1,0:T(8,128)(2,1)}, u32[]{:S(2)}) copy-start(bf16[5120,256]{1,0:T(8,128)(2,1)} %get-tuple-element.178) | copy-start | bytes 7864324 | tf_op jit(solution)/shard_map/while
Sparse Core Ops, SparseCore 0:
  174.5 90.6 all-gather.1
  359.9 94.4 all-reduce.1
where the time goes:
time: 467 us; the launch traced here: 464 us
  other arithmetic  178 us (38%)
  waiting for transfers between devices  169 us (36%)
  local copies, waits for them, and re-layouts  73.9 us (16%)
  matrix products  28.4 us (6%)
  between operations  14.1 us (3%)
    another operation x1, other arithmetic, whiten(): lax.reduce_window(amplitude, jnp.zeros((), amplitude.dtype), lax.add, win...  129 us
    psum x1, waiting for transfers between devices, shards(): summed_hours = lax.psum(partial_stacks, 'hour')  94.6 us
    all_gather x1, waiting for transfers between devices, shards(): gathered = lax.all_gather(local_sources, 'chan', axis=0, tiled=True)  74.7 us
    another operation x6, other arithmetic  34.9 us
    dot_general x1, matrix products, shards(): chosen = jnp.dot(onehot, flattened, preferred_element_type=jnp.float32)  16.1 us
    dot_general x1, local copies, waits for them, and re-layouts, shards(): chosen = jnp.dot(onehot, flattened, preferred_element_type=jnp.float32)  13.8 us
    reshape x1, local copies, waits for them, and re-layouts, shards(): flattened = gathered.reshape(block_count, -1)  13 us
    dot_general x4, matrix products, one_slot(): jnp.dot(cross, table_values, preferred_element_type=jnp.float32)  12.3 us
  transfers between devices with their start and end apart: 2, of which 2 were waited for; matrix products, arithmetic and copies ran while one was open for 3% of the time, Pallas kernels for 0%

commit v1 on v0

--- a/solution.py
+++ b/solution.py
@@ -86,7 +86,7 @@
         return lagged.reshape(VS, block_chans, LAGS)
 
     partial_stacks = lax.map(one_slot, chosen)
-    summed_hours = lax.psum(partial_stacks, "hour")
+    summed_hours = jnp.sum(lax.all_gather(partial_stacks, "hour"), axis=0)
     share = slot_total // hour_count
     return lax.dynamic_slice_in_dim(summed_hours, lax.axis_index("hour") * share, share, 0)
 

time: 467 us -> 536 us (1.15)
  waiting for transfers between devices: 169 us -> 228 us
  other arithmetic: 178 us -> 188 us
    all_gather x0 -> x1, waiting for transfers between devices: none -> 153 us  [shards(): summed_hours = jnp.sum(lax.all_gather(partial_stacks, 'hour'), axis=0)]
    psum x1 -> x0, waiting for transfers between devices: 94.6 us -> none  [shards(): summed_hours = lax.psum(partial_stacks, 'hour')]
    reduce_sum x0 -> x1, other arithmetic: none -> 9.84 us  [shards(): summed_hours = jnp.sum(lax.all_gather(partial_stacks, 'hour'), axis=0)]
where the time goes in v1:
time: 536 us; the launch traced here: 533 us
  waiting for transfers between devices  228 us (43%)
  other arithmetic  188 us (35%)
  local copies, waits for them, and re-layouts  74 us (14%)
  matrix products  28.4 us (5%)
  between operations  13.7 us (3%)
    all_gather x1, waiting for transfers between devices, shards(): summed_hours = jnp.sum(lax.all_gather(partial_stacks, 'hour'), axis=0)  153 us
    another operation x1, other arithmetic, whiten(): lax.reduce_window(amplitude, jnp.zeros((), amplitude.dtype), lax.add, win...  130 us
    all_gather x1, waiting for transfers between devices, shards(): gathered = lax.all_gather(local_sources, 'chan', axis=0, tiled=True)  74.7 us
    another operation x6, other arithmetic  34.9 us
    dot_general x1, matrix products, shards(): chosen = jnp.dot(onehot, flattened, preferred_element_type=jnp.float32)  16.1 us
    dot_general x1, local copies, waits for them, and re-layouts, shards(): chosen = jnp.dot(onehot, flattened, preferred_element_type=jnp.float32)  14 us
    reshape x1, local copies, waits for them, and re-layouts, shards(): flattened = gathered.reshape(block_count, -1)  13 us
    dot_general x4, matrix products, one_slot(): jnp.dot(cross, table_values, preferred_element_type=jnp.float32)  12.3 us
  transfers between devices with their start and end apart: 2, of which 2 were waited for; matrix products, arithmetic and copies ran while one was open for 3% of the time, Pallas kernels for 0%

profile of v1, /device:TPU:1, one launch (start us, length us, event | category | flops | bytes accessed | tf_op | source)
XLA Modules:
  0.0 532.7 jit_solution(10333317314211417057)
XLA Ops:
  6.5 3.2 copy.26
  9.8 0.3 convert_element_type.43
  10.1 2.3 copy-done
  12.4 0.8 add_sqrt_fusion
  13.3 129.6 %reduce_window.7 = f32[2,128,2560]{1,2,0:T(8,128)} reduce-window(f32[2,128,2560]{1,2,0:T(8,128)S(1)} %add_sqrt_fusion, f32[]{:T(128)} %constant.29.clone.1), window={size=1x1x129 pad=0_0x0_0x64_64}, to_apply=%region_2.0 | reduce-window | flops 83886080 | bytes 5242884 | tf_op jit(solution)/shard_map/reduce_window | solution.py:18
  142.8 4.0 divide_convert_fusion.1
  146.8 10.4 %slice.38 = bf16[2,8,2560]{1,2,0:T(8,128)(2,1)} slice(bf16[2,128,2560]{1,2,0:T(8,128)(2,1)S(1)} %get-tuple-element.90), slice={[0:2:1], [0:128:16], [0:2560:1]} | slice | bytes 163840 | tf_op jit(solution)/shard_map/slice | solution.py:58
  157.2 10.2 %slice.39 = bf16[2,8,2560]{1,2,0:T(8,128)(2,1)} slice(bf16[2,128,2560]{1,2,0:T(8,128)(2,1)S(1)} %get-tuple-element.91), slice={[0:2:1], [0:128:16], [0:2560:1]} | slice | bytes 163840 | tf_op jit(solution)/shard_map/slice | solution.py:58
  167.4 3.8 maximum_bitcast_fusion
  171.2 3.5 copy.27
  174.9 0.6 copy.30
  175.5 1.6 copy.31
  177.5 11.7 %cosine_convert_fusion = (bf16[2560,256]{1,0:T(8,128)(2,1)S(1)}, bf16[2560,256]{1,0:T(8,128)(2,1)S(1)}) fusion(s32[256]{0:T(256)S(1)} %compare_select_fusion, s32[2560]{0:T(1024)S(1)} %iota_add_fusion), kind=kLoop, calls=%fused_computation.34 | loop fusion | flops 11141120 | bytes 2632704 | tf_op jit(solution)/shard_map/convert.9
  189.2 1.7 pad_maximum_fusion
  190.9 74.7 %all-gather.4.cloned.1.call-done = bf16[512,2,2,2560]{3,2,1,0:T(2,128)(2,1)} async-done(((bf16[8,2,2,2560]{3,2,1,0:T(2,128)(2,1)}), bf16[512,2,2,2560]{3,2,1,0:T(2,128)(2,1)}) %all-gather.4.cloned.1.call-update) | async-done | bytes 10485776 | tf_op jit(solution)/shard_map/all_gather | solution.py:63
  265.6 13.0 %reshape.97 = bf16[64,81920]{1,0:T(8,128)(2,1)} reshape(bf16[512,2,2,2560]{3,2,1,0:T(2,128)(2,1)} %all-gather.4.cloned.1.call-done) | data formatting | bytes 20971520 | tf_op jit(solution)/shard_map/reshape | solution.py:64
  278.6 14.0 %dot_general.11 = bf16[8,2,2,2560,64]{3,2,1,0,4:T(2,128)(2,1)} reshape(bf16[81920,64]{0,1:T(8,128)(2,1)} %bitcast.72) | data formatting | bytes 20971520 | tf_op jit(solution)/shard_map/dot_general | solution.py:65
  292.6 16.1 %fusion.8 = f32[4,8,2,2,2560]{4,0,3,2,1:T(4,128)} fusion(bf16[8,2,2,2560,64]{3,2,1,0,4:T(2,128)(2,1)} %dot_general.11, s32[64]{0:T(128)S(1)} %add_reduce_fusion, pred[64]{0:T(512)(128)(4,1)S(1)} %fusion.14), kind=kOutput, calls=%fused_computation.19 | convolution fusion | flops 41943552 | bytes 11796800 | tf_op jit(solution)/shard_map/dot_general | solution.py:65
  308.7 51.4 %while.10 = (s32[]{:T(128)}, f32[4,8,128,256]{3,2,1,0:T(8,128)}, f32[4,8,2,2,2560]{4,0,3,2,1:T(4,128)}, bf16[2,128,2560]{2,1,0:T(8,128)(2,1)S(1)}, bf16[2,128,25...) while((s32[]{:T(128)}, f32[4,8,128,256]{3,2,1,0:T(8,128)}, ...), condition=%wide.region_4.5_spmd, body=%wide.region_3.4_spmd.sunk | while | flops 2748841984 | bytes 53281388 | solution.py:88
  308.9 1.7 constant_dynamic-slice_fusion.3
  310.6 0.2 copy.51
  310.7 0.2 fusion.28
  311.0 0.7 bitcast_convert_fusion.5
  311.7 5.8 %add_convert_fusion.2 = (bf16[8,128,2560]{2,1,0:T(8,128)(2,1)S(1)}, bf16[8,128,2560]{2,1,0:T(8,128)(2,1)S(1)}) fusion(f32[128,2560]{1,0:T(8,128)S(1)} %get-tuple-element.145, f32[8,2560]{1,0:T(8,128)S(1)} %get-tuple-element.148, f32[128,2560]{1,0:T(8,128)S(1)} %get-tuple-element.149, f32[8,2560]{1,0:T(8,128)S(1)} %get-tuple-element.150, ...), kind=kLoop, calls=%fused_computation.5.clone.1 | loop fusion | flops 41943040 | bytes 16056320 | tf_op jit(solution)/shard_map/convert.7
  317.5 3.1 fusion.29
  320.6 1.1 constant_dynamic-update-slice_fusion.2
  321.7 1.7 constant_dynamic-slice_fusion.3
  323.4 0.2 copy.51
  323.5 0.2 fusion.28
  323.8 0.7 bitcast_convert_fusion.5
  324.5 5.8 %add_convert_fusion.2 = (bf16[8,128,2560]{2,1,0:T(8,128)(2,1)S(1)}, bf16[8,128,2560]{2,1,0:T(8,128)(2,1)S(1)}) fusion(f32[128,2560]{1,0:T(8,128)S(1)} %get-tuple-element.145, f32[8,2560]{1,0:T(8,128)S(1)} %get-tuple-element.148, f32[128,2560]{1,0:T(8,128)S(1)} %get-tuple-element.149, f32[8,2560]{1,0:T(8,128)S(1)} %get-tuple-element.150, ...), kind=kLoop, calls=%fused_computation.5.clone.1 | loop fusion | flops 41943040 | bytes 16056320 | tf_op jit(solution)/shard_map/convert.7
  330.3 3.1 fusion.29
  333.4 1.1 constant_dynamic-update-slice_fusion.2
  334.5 1.7 constant_dynamic-slice_fusion.3
  336.4 0.2 fusion.28
  336.6 0.7 bitcast_convert_fusion.5
  337.3 5.8 %add_convert_fusion.2 = (bf16[8,128,2560]{2,1,0:T(8,128)(2,1)S(1)}, bf16[8,128,2560]{2,1,0:T(8,128)(2,1)S(1)}) fusion(f32[128,2560]{1,0:T(8,128)S(1)} %get-tuple-element.145, f32[8,2560]{1,0:T(8,128)S(1)} %get-tuple-element.148, f32[128,2560]{1,0:T(8,128)S(1)} %get-tuple-element.149, f32[8,2560]{1,0:T(8,128)S(1)} %get-tuple-element.150, ...), kind=kLoop, calls=%fused_computation.5.clone.1 | loop fusion | flops 41943040 | bytes 16056320 | tf_op jit(solution)/shard_map/convert.7
  343.1 3.1 fusion.29
  346.2 1.1 constant_dynamic-update-slice_fusion.2
  347.3 1.7 constant_dynamic-slice_fusion.3
  349.2 0.2 fusion.28
  349.5 0.7 bitcast_convert_fusion.5
  350.1 5.8 %add_convert_fusion.2 = (bf16[8,128,2560]{2,1,0:T(8,128)(2,1)S(1)}, bf16[8,128,2560]{2,1,0:T(8,128)(2,1)S(1)}) fusion(f32[128,2560]{1,0:T(8,128)S(1)} %get-tuple-element.145, f32[8,2560]{1,0:T(8,128)S(1)} %get-tuple-element.148, f32[128,2560]{1,0:T(8,128)S(1)} %get-tuple-element.149, f32[8,2560]{1,0:T(8,128)S(1)} %get-tuple-element.150, ...), kind=kLoop, calls=%fused_computation.5.clone.1 | loop fusion | flops 41943040 | bytes 16056320 | tf_op jit(solution)/shard_map/convert.7
  356.0 3.1 fusion.29
  359.0 1.1 constant_dynamic-update-slice_fusion.2
  360.2 153.4 %all-gather.6.cloned.1.call-done = f32[16,8,128,256]{3,2,1,0:T(8,128)} async-done(((f32[4,8,128,256]{3,2,1,0:T(8,128)}), f32[16,8,128,256]{3,2,1,0:T(8,128)}) %all-gather.6.cloned.1.call-update) | async-done | bytes 16777232 | tf_op jit(solution)/shard_map/all_gather | solution.py:89
  513.6 9.8 %reduce_sum.9 = f32[4,8,128,256]{3,2,1,0:T(8,128)} reduce(f32[4,4,8,128,256]{4,3,2,1,0:T(8,128)} %bitcast.75, f32[]{:T(128)} %constant.29.clone.1), dimensions={0}, to_apply=%region_5.6 | reduce | flops 3145728 | bytes 20971524 | tf_op jit(solution)/shard_map/reduce_sum | solution.py:89
  523.4 2.3 constant_dynamic-slice_fusion.1
  (37 shorter events, 0.9 us)
Async XLA Ops:
  6.5 259.1 %all-gather.4.cloned.1.call-start = ((), (), s32[]{:S(2)}) async-start(), calls=%async_computation | async-start | bytes 10649600 | tf_op jit(solution)/shard_map/all_gather | solution.py:63
  10.1 2.3 copy-start
  146.8 20.6 %copy-start.1 = (bf16[2,128,2560]{1,2,0:T(8,128)(2,1)}, bf16[2,128,2560]{1,2,0:T(8,128)(2,1)S(1)}, u32[]{:S(2)}) copy-start(bf16[2,128,2560]{1,2,0:T(8,128)(2,1)S(1)} %get-tuple-element.91) | copy-start | bytes 3932164
  174.8 338.8 %all-gather.6.cloned.1.call-start = ((), (), s32[]{:S(2)}) async-start(), calls=%async_computation.1 | async-start | bytes 20971520 | tf_op jit(solution)/shard_map/all_gather | solution.py:89
  174.8 2.3 copy-start.3
  174.8 2.3 copy-start.4
  311.7 5.8 %copy-start.2 = (bf16[5120,256]{1,0:T(8,128)(2,1)S(1)}, bf16[5120,256]{1,0:T(8,128)(2,1)}, u32[]{:S(2)}) copy-start(bf16[5120,256]{1,0:T(8,128)(2,1)} %get-tuple-element.178) | copy-start | bytes 7864324 | tf_op jit(solution)/shard_map/while
  324.5 5.8 %copy-start.2 = (bf16[5120,256]{1,0:T(8,128)(2,1)S(1)}, bf16[5120,256]{1,0:T(8,128)(2,1)}, u32[]{:S(2)}) copy-start(bf16[5120,256]{1,0:T(8,128)(2,1)} %get-tuple-element.178) | copy-start | bytes 7864324 | tf_op jit(solution)/shard_map/while
  337.3 5.8 %copy-start.2 = (bf16[5120,256]{1,0:T(8,128)(2,1)S(1)}, bf16[5120,256]{1,0:T(8,128)(2,1)}, u32[]{:S(2)}) copy-start(bf16[5120,256]{1,0:T(8,128)(2,1)} %get-tuple-element.178) | copy-start | bytes 7864324 | tf_op jit(solution)/shard_map/while
  350.1 5.8 %copy-start.2 = (bf16[5120,256]{1,0:T(8,128)(2,1)S(1)}, bf16[5120,256]{1,0:T(8,128)(2,1)}, u32[]{:S(2)}) copy-start(bf16[5120,256]{1,0:T(8,128)(2,1)} %get-tuple-element.178) | copy-start | bytes 7864324 | tf_op jit(solution)/shard_map/while
Sparse Core Ops, SparseCore 0:
  174.9 90.6 all-gather.3
  360.3 153.2 all-gather.5
